TPU v7x, 32 devices: a whole 2x2x4 slice. The times are simulated.
32 devices in a mesh: seg: 4 (over y, core), ep: 8 (over z, x).
Axes of the slice: x: 2, y: 2, z: 4, core: 2. Of those that a mesh axis runs over, the one named last changes fastest.
Arguments:
- queries: bfloat16 [2048, 2048], P(('seg', 'ep')), may hold values from -6 to 6
- keys: bfloat16 [2048, 2048], P(('seg', 'ep')), may hold values from -1.25 to 1.25
- values: bfloat16 [2048, 2048], P(('seg', 'ep')), may hold values from -54 to 54
- log_decay: float32 [2048, 16], P('seg', 'ep'), may hold values from -1 to 0
- out_gain: float32 [2048], replicated, may hold values from 0.1 to 1.9
- out_proj: bfloat16 [2048, 6144], P('ep', 'seg'), may hold values from -0.125 to 0.125
- experts: int32 [256, 2], P(('seg', 'ep')), may hold values from 0 to 3, all different within a row; in each aligned block of 8 rows (0 to 7, 8 to 15, ...) at most 8 rows name the same one
- gates: float32 [256, 2], P(('seg', 'ep')), may hold values from 0.2 to 1
- up_weight: bfloat16 [8, 6144, 2304], P('ep', None, 'seg'), may hold values from -0.078125 to 0.078125
- down_weight: bfloat16 [8, 2304, 6144], P('ep', 'seg'), may hold values from -0.09375 to 0.09375
Outputs:
- attn_out: bfloat16 [2048, 2048], P(('seg', 'ep'))
- moe_out: bfloat16 [256, 6144], P(('seg', 'ep'))
Inputs may be any that keep to these rules, and one draw needn't show every extreme that they name: Each row names two different experts. The 8 rows of one device name any one expert at most 8 times, and in some devices one expert exactly 8 times.
All inputs are finite; a program needn't handle non-finite values.
Results may differ from a plain program's by a relative error of at most 0.025.
Values may be sent and summed in bfloat16 or wider, within the bound.
A program may use at most 128 MiB of HBM per device.

v0:
```python
import math
import jax
import jax.numpy as jnp
from jax import lax
from jax.sharding import PartitionSpec as P

epsilon = 1e-06


def prefix(x, axis, join, neutral):
    place = lax.axis_index(axis)
    gathered = jax.tree.map(
        lambda a, kind: lax.all_gather(a.astype(kind), axis), x, (jnp.bfloat16, jnp.bfloat16)
    )
    state = jax.tree.map(lambda a, e: jnp.zeros_like(a) + jnp.asarray(e, a.dtype), x, neutral)

    def one(turn, state):
        return join(
            state,
            jax.tree.map(
                lambda a, own: lax.dynamic_index_in_dim(a, turn, 0, False).astype(own.dtype),
                gathered,
                x,
            ),
        )

    return lax.fori_loop(0, place, one, state)


def chain_combine(first_part, second_part):
    return (
        first_part[0] * second_part[0],
        second_part[0][:, None, None] * first_part[1] + second_part[1],
    )


def route_tables(experts, gates, expert_count, capacity):
    token_count = experts.shape[0]
    flattened = experts.reshape(-1)
    onehot = (flattened[:, None] == jnp.arange(expert_count, dtype=jnp.int32)[None, :]).astype(
        jnp.int32
    )
    earlier = jnp.cumsum(onehot, axis=0) - onehot
    position = jnp.sum(earlier * onehot, axis=1)
    slot_index = (flattened * capacity + position).reshape(token_count, 2)
    columns = jnp.arange(expert_count * capacity, dtype=jnp.int32)
    matches = slot_index[:, :, None] == columns[None, None, :]
    dispatch = jnp.any(matches, axis=1).T.astype(jnp.bfloat16)
    combine = jnp.sum(jnp.where(matches, gates[:, :, None], 0.0), axis=1)
    return (dispatch, combine)


def expert_output(row_data, up_piece, down_piece):
    hidden = jax.nn.silu(jnp.dot(row_data, up_piece, preferred_element_type=jnp.float32)).astype(
        jnp.bfloat16
    )
    return jnp.dot(hidden, down_piece, preferred_element_type=jnp.float32)


def on_device(
    queries, keys, values, log_decay, out_gain, out_proj, experts, gates, up_weight, down_weight
):
    highest = lax.Precision.HIGHEST
    ep_count = lax.axis_size("ep")
    heads_local = log_decay.shape[1]
    head_dim = queries.shape[1] // (heads_local * ep_count)
    query_heads, key_heads, value_heads = (
        lax.all_to_all(queries, "ep", split_axis=1, concat_axis=0, tiled=True),
        lax.all_to_all(keys, "ep", split_axis=1, concat_axis=0, tiled=True),
        lax.all_to_all(values, "ep", split_axis=1, concat_axis=0, tiled=True),
    )
    seg_length = query_heads.shape[0]
    query_heads = query_heads.reshape(seg_length, heads_local, head_dim)
    key_heads = key_heads.reshape(seg_length, heads_local, head_dim)
    value_heads = value_heads.reshape(seg_length, heads_local, head_dim)
    cumulative = jnp.cumsum(log_decay, axis=0)
    across = cumulative.T
    block_size = math.gcd(seg_length, 512)
    starts = jnp.arange(seg_length // block_size, dtype=jnp.int32) * block_size
    token_positions = jnp.arange(seg_length, dtype=jnp.int32)

    def block_mix(start):
        query_block = lax.dynamic_slice_in_dim(query_heads, start, block_size, 0)
        cum_block = lax.dynamic_slice_in_dim(across, start, block_size, 1)
        row_ids = start + jnp.arange(block_size, dtype=jnp.int32)
        causal = (row_ids[:, None] >= token_positions[None, :])[None]
        log_gap = cum_block[:, :, None] - across[:, None, :]
        weight = jnp.where(causal, jnp.exp(jnp.where(causal, log_gap, 0.0)), 0.0)
        scores = jnp.einsum(
            "thd,shd->hts", query_block, key_heads, preferred_element_type=jnp.float32
        )
        mixing = (scores * weight).astype(jnp.bfloat16)
        return jnp.einsum("hts,she->the", mixing, value_heads, preferred_element_type=jnp.float32)

    inside = lax.map(block_mix, starts).reshape(seg_length, heads_local, head_dim)
    ending = cumulative[-1]
    to_end = jnp.exp(ending[None, :] - cumulative)
    key_float = key_heads.astype(jnp.float32)
    value_float = value_heads.astype(jnp.float32)
    local_state = jnp.einsum("sh,shd,she->hde", to_end, key_float, value_float, precision=highest)
    identity = (jnp.ones_like(ending), jnp.zeros_like(local_state))
    carried = prefix((jnp.exp(ending), local_state), "seg", chain_combine, identity)[1]
    outside = jnp.exp(cumulative)[:, :, None] * jnp.einsum(
        "thd,hde->the", query_heads.astype(jnp.float32), carried, precision=highest
    )
    mixture = (inside + outside).astype(jnp.bfloat16).reshape(seg_length, heads_local * head_dim)
    token_mix = lax.all_to_all(mixture, "ep", split_axis=0, concat_axis=1, tiled=True)
    as_float = token_mix.astype(jnp.float32)
    inv_rms = lax.rsqrt(jnp.mean(as_float * as_float, axis=1, keepdims=True) + epsilon)
    attn_out = (as_float * inv_rms * out_gain[None, :]).astype(jnp.bfloat16)
    row_stride = 8
    own_width = heads_local * head_dim
    feature_count = own_width * ep_count
    picked_float = mixture.reshape(seg_length // row_stride, row_stride, own_width)[:, 0].astype(
        jnp.float32
    )
    square_sums = lax.psum(jnp.sum(picked_float * picked_float, axis=1), "ep")
    picked_rms = lax.rsqrt(square_sums[:, None] / feature_count + epsilon)
    gain_slice = lax.dynamic_slice_in_dim(out_gain, lax.axis_index("ep") * own_width, own_width, 0)
    normed_rows = (picked_float * picked_rms * gain_slice[None, :]).astype(jnp.bfloat16)
    proj_terms = jnp.dot(
        normed_rows,
        lax.all_gather(out_proj, "seg", axis=1, tiled=True),
        preferred_element_type=jnp.float32,
    )
    moe_in = lax.psum_scatter(
        proj_terms.astype(jnp.bfloat16), "ep", scatter_dimension=0, tiled=True
    )
    expert_count = ep_count // 2
    token_count, model_width = moe_in.shape
    capacity = max(2, 4 * token_count // expert_count)
    dispatch, combine = route_tables(experts, gates, expert_count, capacity)
    up_piece = up_weight[0]
    down_piece = down_weight[0]
    slot_rows = jnp.dot(dispatch, moe_in, preferred_element_type=jnp.float32).astype(jnp.bfloat16)
    outgoing = jnp.repeat(slot_rows.reshape(expert_count, capacity, model_width), 2, axis=0)
    arrived = lax.all_to_all(outgoing, "ep", split_axis=0, concat_axis=0, tiled=True).reshape(
        ep_count * capacity, model_width
    )
    gathered = lax.all_gather(arrived, "seg", axis=0, tiled=True)
    owned_sums = lax.psum_scatter(
        expert_output(gathered, up_piece, down_piece).astype(jnp.bfloat16),
        "seg",
        scatter_dimension=0,
        tiled=True,
    ).astype(jnp.float32)
    returned_back = lax.all_to_all(
        owned_sums.reshape(ep_count, capacity, model_width).astype(jnp.bfloat16),
        "ep",
        split_axis=0,
        concat_axis=0,
        tiled=True,
    ).astype(jnp.float32)
    paired = returned_back.reshape(expert_count, 2, capacity, model_width)
    halves = (paired[:, 0] + paired[:, 1]).reshape(expert_count * capacity, model_width)
    summed = jnp.dot(combine, halves, precision=highest)
    moe_out = summed.astype(jnp.bfloat16)
    return (attn_out, moe_out)


def solution(mesh):
    placed = (
        P(("seg", "ep"), None),
        P(("seg", "ep"), None),
        P(("seg", "ep"), None),
        P("seg", "ep"),
        P(),
        P("ep", "seg"),
        P(("seg", "ep"), None),
        P(("seg", "ep"), None),
        P("ep", None, "seg"),
        P("ep", "seg", None),
    )
    return jax.shard_map(
        on_device,
        mesh=mesh,
        in_specs=placed,
        out_specs=(P(("seg", "ep"), None), P(("seg", "ep"), None)),
        check_vma=False,
    )
```

profile of v0, /device:TPU:0, one launch (start us, length us, event | category | flops | bytes accessed | tf_op | source)
XLA Modules:
  0.0 282.9 jit_solution(439262611105810195)
XLA Ops:
  7.2 1.7 copy.181
  8.8 7.3 %all-to-all-start.1 = ((bf16[64,8,256]{2,0,1:T(8,128)(2,1)}), bf16[64,8,256]{2,0,1:T(8,128)(2,1)S(1)}, u32[]{:S(2)}, u32[]{:S(2)}) async-start(bf16[64,8,256]{2,0,1:T(8,128)(2,1)} %bitcast.87), calls=%async_computation.1 | async-start | bytes 524288 | tf_op jit(solution)/shard_map/all_to_all | solution.py:69
  16.1 1.7 copy.180
  17.8 7.2 %all-to-all-done.1 = bf16[64,8,256]{2,0,1:T(8,128)(2,1)S(1)} async-done(((bf16[64,8,256]{2,0,1:T(8,128)(2,1)}), bf16[64,8,256]{2,0,1:T(8,128)(2,1)S(1)}, u32[]{:S(2)}, u32[]{:S(2)}) %all-to-all-start.1) | async-done | bytes 262176 | tf_op jit(solution)/shard_map/all_to_all | solution.py:69
  25.0 3.6 %all-to-all-start.2 = ((bf16[64,8,256]{2,0,1:T(8,128)(2,1)}), bf16[64,8,256]{2,0,1:T(8,128)(2,1)S(1)}, u32[]{:S(2)}, u32[]{:S(2)}) async-start(bf16[64,8,256]{2,0,1:T(8,128)(2,1)} %bitcast.86), calls=%async_computation.2 | async-start | bytes 524288 | tf_op jit(solution)/shard_map/all_to_all | solution.py:70
  28.6 0.0 all-gather.5.cloned.1.call-start
  28.7 0.7 all-gather.5.cloned.1.call-update
  29.4 0.7 reshape.132
  30.1 0.6 reduce-window.6
  30.7 0.2 slice_reduce_fusion
  30.8 0.2 reduce-window.9
  31.0 0.1 add_bitcast_fusion
  31.1 1.7 copy.182
  32.8 4.4 %all-to-all-done.2 = bf16[64,8,256]{2,0,1:T(8,128)(2,1)S(1)} async-done(((bf16[64,8,256]{2,0,1:T(8,128)(2,1)}), bf16[64,8,256]{2,0,1:T(8,128)(2,1)S(1)}, u32[]{:S(2)}, u32[]{:S(2)}) %all-to-all-start.2) | async-done | bytes 262176 | tf_op jit(solution)/shard_map/all_to_all | solution.py:70
  37.2 3.6 %all-to-all-start = ((bf16[64,8,256]{2,0,1:T(8,128)(2,1)}), bf16[64,8,256]{2,0,1:T(8,128)(2,1)S(1)}, u32[]{:S(2)}, u32[]{:S(2)}) async-start(bf16[64,8,256]{2,0,1:T(8,128)(2,1)} %bitcast.88), calls=%async_computation | async-start | bytes 524288 | tf_op jit(solution)/shard_map/all_to_all | solution.py:68
  40.8 0.0 reduce-scatter.3.cloned.1.call-start
  40.8 0.2 fusion.38
  41.0 5.2 %all-gather.1 = bf16[4,1,2]{2,1,0:T(2,128)(2,1)S(1)} all-gather(bf16[1,1,2]{2,1,0:T(2,128)(2,1)S(1)} %bitcast.114), channel_id=1, replica_groups=mesh['seg'=4,'ep'=8] {'seg'}, dimensions={0}, use_global_device_ids=true | all-gather | bytes 20 | tf_op jit(solution)/shard_map/all_gather | solution.py:13
  46.2 0.2 slice_reduce_fusion.1
  46.4 0.1 bitcast_exponential_fusion
  46.5 0.2 copy.131
  46.6 0.1 copy.130
  46.8 0.1 dynamic_slice.20
  46.8 0.1 iota_compare_fusion
  46.9 0.1 reshape.131
  47.0 0.1 reshape.134
  47.1 2.3 all-to-all-done
  49.3 0.1 reshape.130
  49.4 0.6 convert_multiply_fusion.1
  50.0 0.6 convolution_convert_fusion.4
  50.6 7.7 %all-gather = bf16[8,128,128]{2,1,0:T(8,128)(2,1)S(1)} all-gather(bf16[2,128,128]{2,1,0:T(8,128)(2,1)S(1)} %convolution_convert_fusion.4), channel_id=2, replica_groups=mesh['seg'=4,'ep'=8] {'seg'}, dimensions={0}, use_global_device_ids=true | all-gather | bytes 327680 | tf_op jit(solution)/shard_map/all_gather | solution.py:13
  58.3 1.0 fusion.5
  59.4 0.4 fusion.8
  59.8 0.3 copy.138
  60.0 0.2 reshape_reshape.3
  60.3 0.1 fusion.30
  60.4 19.6 %psum.7 = f32[64]{0:T(128)S(1)} all-reduce(f32[64]{0:T(128)S(1)} %fusion.30), channel_id=1, replica_groups=mesh['seg'=4,'ep'=8] {'ep'}, use_global_device_ids=true, to_apply=%region_10.11 | all-reduce | flops 64 | bytes 512 | tf_op jit(solution)/shard_map/psum | solution.py:117
  80.0 3.5 %convolution_convert_fusion.1 = bf16[64,6144]{1,0:T(8,128)(2,1)} fusion(bf16[256,6144]{1,0:T(8,128)(2,1)} %all-gather.5.cloned.1.call-done, f32[64,1,256]{2,1,0:T(1,128)S(1)} %slice_convert_fusion, f32[256]{0:T(256)S(1)} %dynamic_slice.20, f32[64]{0:T(128)S(1)} %add_rsqrt_fusion), kind=kOutput, calls=%fused_computation.7 | convolution fusion | flops 201768960 | bytes 3998976 | tf_op jit(solution)/shard_map/dot_general | solution.py:121
  83.5 0.0 all-gather.7.cloned.1.call-start
  83.5 0.1 copy.140
  83.6 0.1 eq.28
  83.7 0.1 fusion.37
  83.8 0.2 select_reduce_fusion.1
  84.0 0.1 reduce_sum.40
  84.1 0.1 copy.142
  84.2 0.1 fusion.36
  84.3 60.6 %reduce-scatter.3.cloned.1.call-done = bf16[8,6144]{1,0:T(8,128)(2,1)} async-done(((bf16[64,6144]{1,0:T(8,128)(2,1)}), bf16[8,6144]{1,0:T(8,128)(2,1)}) %reduce-scatter.3.cloned.1.call-update) | async-done | bytes 98320 | tf_op jit(solution)/shard_map/reduce_scatter | solution.py:126
  144.8 1.2 fusion.3
  146.0 0.1 broadcast_in_dim.69
  146.1 21.9 %all_to_all.71 = bf16[8,8,6144]{2,1,0:T(8,128)(2,1)} all-to-all(bf16[8,8,6144]{2,1,0:T(8,128)(2,1)S(1)} %bitcast.97), channel_id=1, replica_groups=mesh['seg'=4,'ep'=8] {'ep'}, dimensions={0} | all-to-all | bytes 1572864 | tf_op jit(solution)/shard_map/all_to_all | solution.py:137
  168.0 0.0 all-gather.7.cloned.1.call-update
  168.0 0.2 reduce-scatter.5.cloned.1.call-start
  168.2 27.4 %all-gather.7.cloned.1.call-done = bf16[256,6144]{1,0:T(8,128)(2,1)} async-done(((bf16[64,6144]{1,0:T(8,128)(2,1)}), bf16[256,6144]{1,0:T(8,128)(2,1)}) %all-gather.7.cloned.1.call-update) | async-done | bytes 3145744 | tf_op jit(solution)/shard_map/all_gather | solution.py:140
  195.6 15.9 %convolution_convert_fusion = bf16[256,6144]{1,0:T(8,128)(2,1)} fusion(bf16[1,576,6144]{2,1,0:T(8,128)(2,1)} %param.21, bf16[256,6144]{1,0:T(8,128)(2,1)} %all-gather.7.cloned.1.call-done, bf16[1,6144,576]{1,2,0:T(8,128)(2,1)} %param.20), kind=kOutput, calls=%fused_computation.3 | convolution fusion | flops 3626188800 | bytes 20447232 | tf_op jit(solution)/shard_map/dot_general | solution.py:57
  211.5 0.2 all_to_all.61
  211.7 14.6 %all_to_all.72 = bf16[8,64,256]{2,1,0:T(8,128)(2,1)S(1)} all-to-all(bf16[8,64,256]{2,1,0:T(8,128)(2,1)S(1)} %all_to_all.61), channel_id=1, replica_groups=mesh['seg'=4,'ep'=8] {'ep'}, dimensions={0} | all-to-all | bytes 524288 | tf_op jit(solution)/shard_map/all_to_all | solution.py:107
  226.3 23.2 %reduce-scatter.5.cloned.1.call-done = bf16[64,6144]{1,0:T(8,128)(2,1)} async-done(((bf16[256,6144]{1,0:T(8,128)(2,1)}), bf16[64,6144]{1,0:T(8,128)(2,1)}) %reduce-scatter.5.cloned.1.call-update) | async-done | bytes 786448 | tf_op jit(solution)/shard_map/reduce_scatter | solution.py:141
  249.5 5.5 %all-to-all-start.5 = ((bf16[8,8,6144]{2,1,0:T(8,128)(2,1)}), bf16[8,8,6144]{2,1,0:T(8,128)(2,1)S(1)}, u32[]{:S(2)}, u32[]{:S(2)}) async-start(bf16[8,8,6144]{2,1,0:T(8,128)(2,1)} %bitcast.104), calls=%async_computation.7 | async-start | bytes 1572864 | tf_op jit(solution)/shard_map/all_to_all | solution.py:147
  255.1 0.1 select_reduce_fusion
  255.2 0.2 fusion.20
  255.4 0.8 multiply_convert_fusion.2
  256.2 18.9 %all-to-all-done.5 = bf16[8,8,6144]{2,1,0:T(8,128)(2,1)S(1)} async-done(((bf16[8,8,6144]{2,1,0:T(8,128)(2,1)}), bf16[8,8,6144]{2,1,0:T(8,128)(2,1)S(1)}, u32[]{:S(2)}, u32[]{:S(2)}) %all-to-all-start.5) | async-done | bytes 786464 | tf_op jit(solution)/shard_map/all_to_all | solution.py:147
  275.1 0.1 convert.7
  275.2 1.2 convolution_convert_fusion.3
  (19 shorter events, 0.3 us)
Async XLA Ops:
  7.2 39.6 %copy-start = (f32[2048]{0:T(1024)S(1)}, f32[2048]{0:T(1024)}, u32[]{:S(2)}) copy-start(f32[2048]{0:T(1024)} %param.16) | copy-start | bytes 24580
  8.8 16.2 %all-to-all-start.1 = ((bf16[64,8,256]{2,0,1:T(8,128)(2,1)}), bf16[64,8,256]{2,0,1:T(8,128)(2,1)S(1)}, u32[]{:S(2)}, u32[]{:S(2)}) async-start(bf16[64,8,256]{2,0,1:T(8,128)(2,1)} %bitcast.87), calls=%async_computation.1 | async-start | bytes 524288 | tf_op jit(solution)/shard_map/all_to_all | solution.py:69
  25.0 12.2 %all-to-all-start.2 = ((bf16[64,8,256]{2,0,1:T(8,128)(2,1)}), bf16[64,8,256]{2,0,1:T(8,128)(2,1)S(1)}, u32[]{:S(2)}, u32[]{:S(2)}) async-start(bf16[64,8,256]{2,0,1:T(8,128)(2,1)} %bitcast.86), calls=%async_computation.2 | async-start | bytes 524288 | tf_op jit(solution)/shard_map/all_to_all | solution.py:70
  28.6 51.3 %all-gather.5.cloned.1.call-start = ((), (), s32[]{:S(2)}) async-start(), calls=%async_computation.8 | async-start | bytes 3932160 | tf_op jit(solution)/shard_map/all_gather | solution.py:123
  37.2 12.1 %all-to-all-start = ((bf16[64,8,256]{2,0,1:T(8,128)(2,1)}), bf16[64,8,256]{2,0,1:T(8,128)(2,1)S(1)}, u32[]{:S(2)}, u32[]{:S(2)}) async-start(bf16[64,8,256]{2,0,1:T(8,128)(2,1)} %bitcast.88), calls=%async_computation | async-start | bytes 524288 | tf_op jit(solution)/shard_map/all_to_all | solution.py:68
  40.8 104.1 %reduce-scatter.3.cloned.1.call-start = ((), (), s32[]{:S(2)}) async-start(), calls=%async_computation.9 | async-start | bytes 884736 | tf_op jit(solution)/shard_map/reduce_scatter | solution.py:126
  59.8 23.8 %copy-start.1 = (s32[8,2]{0,1:T(2,128)S(1)}, s32[8,2]{0,1:T(2,128)}, u32[]{:S(2)}) copy-start(s32[8,2]{0,1:T(2,128)} %param.18) | copy-start | bytes 196
  83.5 112.1 %all-gather.7.cloned.1.call-start = ((), (), s32[]{:S(2)}) async-start(), calls=%async_computation.10 | async-start | bytes 3932160 | tf_op jit(solution)/shard_map/all_gather | solution.py:140
  168.0 81.5 %reduce-scatter.5.cloned.1.call-start = ((), (), s32[]{:S(2)}) async-start(), calls=%async_computation.11 | async-start | bytes 3932160 | tf_op jit(solution)/shard_map/reduce_scatter | solution.py:141
  211.5 43.6 %copy-start.2 = (f32[8,2]{0,1:T(2,128)S(1)}, f32[8,2]{0,1:T(2,128)}, u32[]{:S(2)}) copy-start(f32[8,2]{0,1:T(2,128)} %param.19) | copy-start | bytes 196
  249.5 25.6 %all-to-all-start.5 = ((bf16[8,8,6144]{2,1,0:T(8,128)(2,1)}), bf16[8,8,6144]{2,1,0:T(8,128)(2,1)S(1)}, u32[]{:S(2)}, u32[]{:S(2)}) async-start(bf16[8,8,6144]{2,1,0:T(8,128)(2,1)} %bitcast.104), calls=%async_computation.7 | async-start | bytes 1572864 | tf_op jit(solution)/shard_map/all_to_all | solution.py:147
Sparse Core Ops, SparseCore 0:
  31.0 31.3 all-gather.4
  83.6 61.1 reduce-scatter.2
  168.1 27.4 all-gather.6
  211.6 37.8 reduce-scatter.4
where the time goes:
time: 284 us; the launch traced here: 283 us
  waiting for transfers between devices  145 us (51%)
  blocking collectives  69 us (24%)
  matrix products  23.7 us (8%)
  starting transfers between devices  20.3 us (7%)
  between operations  14 us (5%)
  local copies, waits for them, and re-layouts  7.68 us (3%)
  other arithmetic  3.54 us (1%)
    reduce_scatter x1, waiting for transfers between devices, on_device(): lax.psum_scatter(proj_terms.astype(jnp.bfloat16), 'ep', scatter_dimension...  60.6 us
    all_gather x1, waiting for transfers between devices, on_device(): gathered = lax.all_gather(arrived, 'seg', axis=0, tiled=True)  27.4 us
    reduce_scatter x1, waiting for transfers between devices, on_device(): lax.psum_scatter(expert_output(gathered, up_piece, down_piece).astype(jnp...  23.2 us
    all_to_all x1, blocking collectives, on_device(): lax.all_to_all(outgoing, 'ep', split_axis=0, concat_axis=0, tiled=True)  21.9 us
    psum x1, blocking collectives, on_device(): square_sums = lax.psum(jnp.sum(picked_float * picked_float, axis=1), 'ep')  19.6 us
    all_to_all x1, waiting for transfers between devices, on_device(): lax.all_to_all(owned_sums.reshape(ep_count, capacity, model_width).astype...  18.9 us
    dot_general x1, matrix products, expert_output(): return jnp.dot(hidden, down_piece, preferred_element_type=jnp.float32)  15.9 us
    all_to_all x1, blocking collectives, on_device(): lax.all_to_all(mixture, 'ep', split_axis=0, concat_axis=1, tiled=True)  14.6 us
  transfers between devices with their start and end apart: 8, of which 7 were waited for; matrix products, arithmetic and copies ran while one was open for 4% of the time, Pallas kernels for 0%

commit v1 on v0

--- a/solution.py
+++ b/solution.py
@@ -60,6 +60,23 @@
 def on_device(
     queries, keys, values, log_decay, out_gain, out_proj, experts, gates, up_weight, down_weight
 ):
+
+    def limits_check(arr):
+        mesh_ax = "seg"
+        total_devices = lax.axis_size(mesh_ax)
+        d_next = arr
+        pages = [d_next]
+        block_next = list(map(lambda k0: (k0 - 1, k0), range(1, total_devices))) + [
+            (total_devices - 1, 0)
+        ]
+        kk = 0
+        while kk < total_devices - 1:
+            d_next = lax.ppermute(d_next, mesh_ax, block_next)
+            pages += [d_next]
+            kk = kk + 1
+        spare = jnp.concatenate([*reversed(pages)], axis=0)
+        return jnp.roll(spare, shift=(lax.axis_index(mesh_ax) + 1) * d_next.shape[0], axis=0)
+
     highest = lax.Precision.HIGHEST
     ep_count = lax.axis_size("ep")
     heads_local = log_decay.shape[1]
@@ -137,7 +154,7 @@
     arrived = lax.all_to_all(outgoing, "ep", split_axis=0, concat_axis=0, tiled=True).reshape(
         ep_count * capacity, model_width
     )
-    gathered = lax.all_gather(arrived, "seg", axis=0, tiled=True)
+    gathered = limits_check(arrived)
     owned_sums = lax.psum_scatter(
         expert_output(gathered, up_piece, down_piece).astype(jnp.bfloat16),
         "seg",

time: 284 us -> 297 us (1.046)
  local copies, waits for them, and re-layouts: 7.68 us -> 15.9 us
  waiting for transfers between devices: 145 us -> 153 us
    ppermute x0 -> x3, waiting for transfers between devices: none -> 34.2 us  [limits_check(): d_next = lax.ppermute(d_next, mesh_ax, block_next)]
    all_gather x1 -> x0, waiting for transfers between devices: 27.4 us -> none  [on_device(): gathered = lax.all_gather(arrived, 'seg', axis=0, tiled=True)]
    unnamed x8 -> x15, local copies, waits for them, and re-layouts: 0.1 us -> 6.69 us
  transfers between devices with their start and end apart: 8 -> 10, of which waited for: 7 -> 9; matrix products, arithmetic and copies ran while one was open for 4% -> 4% of each run, Pallas kernels for 0% -> 0%
where the time goes in v1:
time: 297 us
  waiting for transfers between devices  153 us (52%)
  blocking collectives  66.6 us (22%)
  matrix products  23.7 us (8%)
  starting transfers between devices  20.1 us (7%)
  local copies, waits for them, and re-layouts  15.9 us (5%)
  between operations  13.9 us (5%)
  other arithmetic  3.54 us (1%)
    reduce_scatter x1, waiting for transfers between devices, on_device(): lax.psum_scatter(proj_terms.astype(jnp.bfloat16), 'ep', scatter_dimension...  60.5 us
    ppermute x3, waiting for transfers between devices, limits_check(): d_next = lax.ppermute(d_next, mesh_ax, block_next)  34.2 us
    reduce_scatter x1, waiting for transfers between devices, on_device(): lax.psum_scatter(expert_output(gathered, up_piece, down_piece).astype(jnp...  25.1 us
    all_to_all x1, blocking collectives, on_device(): lax.all_to_all(outgoing, 'ep', split_axis=0, concat_axis=0, tiled=True)  21.7 us
    psum x1, blocking collectives, on_device(): square_sums = lax.psum(jnp.sum(picked_float * picked_float, axis=1), 'ep')  20.3 us
    all_to_all x1, waiting for transfers between devices, on_device(): lax.all_to_all(owned_sums.reshape(ep_count, capacity, model_width).astype...  18.9 us
    dot_general x1, matrix products, expert_output(): return jnp.dot(hidden, down_piece, preferred_element_type=jnp.float32)  15.9 us
    all_gather x2, blocking collectives, prefix(): lax.all_gather(a.astype(kind), axis)  12.9 us
  transfers between devices with their start and end apart: 10, of which 9 were waited for; matrix products, arithmetic and copies ran while one was open for 4% of the time, Pallas kernels for 0%

profile of v1, /device:TPU:0, one launch (start us, length us, event | category | flops | bytes accessed | tf_op | source)
XLA Modules:
  0.0 296.6 jit_solution(9698633333152036990)
XLA Ops:
  7.2 1.7 copy.181
  8.8 7.3 %all-to-all-start.1 = ((bf16[64,8,256]{2,0,1:T(8,128)(2,1)}), bf16[64,8,256]{2,0,1:T(8,128)(2,1)S(1)}, u32[]{:S(2)}, u32[]{:S(2)}) async-start(bf16[64,8,256]{2,0,1:T(8,128)(2,1)} %bitcast.88), calls=%async_computation.1 | async-start | bytes 524288 | tf_op jit(solution)/shard_map/all_to_all | solution.py:86
  16.1 1.7 copy.180
  17.8 7.2 %all-to-all-done.1 = bf16[64,8,256]{2,0,1:T(8,128)(2,1)S(1)} async-done(((bf16[64,8,256]{2,0,1:T(8,128)(2,1)}), bf16[64,8,256]{2,0,1:T(8,128)(2,1)S(1)}, u32[]{:S(2)}, u32[]{:S(2)}) %all-to-all-start.1) | async-done | bytes 262176 | tf_op jit(solution)/shard_map/all_to_all | solution.py:86
  25.0 3.6 %all-to-all-start.2 = ((bf16[64,8,256]{2,0,1:T(8,128)(2,1)}), bf16[64,8,256]{2,0,1:T(8,128)(2,1)S(1)}, u32[]{:S(2)}, u32[]{:S(2)}) async-start(bf16[64,8,256]{2,0,1:T(8,128)(2,1)} %bitcast.87), calls=%async_computation.2 | async-start | bytes 524288 | tf_op jit(solution)/shard_map/all_to_all | solution.py:87
  28.7 0.7 all-gather.4.cloned.1.call-update
  29.4 0.7 reshape.132
  30.1 0.6 reduce-window.6
  30.7 0.2 slice_reduce_fusion
  30.8 0.2 reduce-window.9
  31.0 0.1 add_bitcast_fusion
  31.1 1.7 copy.182
  32.8 4.4 %all-to-all-done.2 = bf16[64,8,256]{2,0,1:T(8,128)(2,1)S(1)} async-done(((bf16[64,8,256]{2,0,1:T(8,128)(2,1)}), bf16[64,8,256]{2,0,1:T(8,128)(2,1)S(1)}, u32[]{:S(2)}, u32[]{:S(2)}) %all-to-all-start.2) | async-done | bytes 262176 | tf_op jit(solution)/shard_map/all_to_all | solution.py:87
  37.2 3.6 %all-to-all-start = ((bf16[64,8,256]{2,0,1:T(8,128)(2,1)}), bf16[64,8,256]{2,0,1:T(8,128)(2,1)S(1)}, u32[]{:S(2)}, u32[]{:S(2)}) async-start(bf16[64,8,256]{2,0,1:T(8,128)(2,1)} %bitcast.89), calls=%async_computation | async-start | bytes 524288 | tf_op jit(solution)/shard_map/all_to_all | solution.py:85
  40.8 0.2 fusion.38
  41.0 5.2 %all-gather.1 = bf16[4,1,2]{2,1,0:T(2,128)(2,1)S(1)} all-gather(bf16[1,1,2]{2,1,0:T(2,128)(2,1)S(1)} %bitcast.115), channel_id=1, replica_groups=mesh['seg'=4,'ep'=8] {'seg'}, dimensions={0}, use_global_device_ids=true | all-gather | bytes 20 | tf_op jit(solution)/shard_map/all_gather | solution.py:13
  46.2 0.2 slice_reduce_fusion.1
  46.4 0.1 bitcast_exponential_fusion
  46.5 0.2 copy.131
  46.6 0.1 copy.130
  46.7 0.8 dynamic_slice.24
  47.5 0.1 iota_compare_fusion
  47.7 1.6 all-to-all-done
  49.4 0.6 convert_multiply_fusion.1
  50.0 0.6 convolution_convert_fusion.4
  50.6 7.7 %all-gather = bf16[8,128,128]{2,1,0:T(8,128)(2,1)S(1)} all-gather(bf16[2,128,128]{2,1,0:T(8,128)(2,1)S(1)} %convolution_convert_fusion.4), channel_id=2, replica_groups=mesh['seg'=4,'ep'=8] {'seg'}, dimensions={0}, use_global_device_ids=true | all-gather | bytes 327680 | tf_op jit(solution)/shard_map/all_gather | solution.py:13
  58.3 1.0 fusion.6
  59.3 0.4 fusion.9
  59.7 0.3 copy.138
  60.0 0.2 reshape_reshape.3
  60.2 0.1 fusion.30
  60.3 20.3 %psum.7 = f32[64]{0:T(128)S(1)} all-reduce(f32[64]{0:T(128)S(1)} %fusion.30), channel_id=1, replica_groups=mesh['seg'=4,'ep'=8] {'ep'}, use_global_device_ids=true, to_apply=%region_10.11 | all-reduce | flops 64 | bytes 512 | tf_op jit(solution)/shard_map/psum | solution.py:134
  80.6 3.5 %convolution_convert_fusion.1 = bf16[64,6144]{1,0:T(8,128)(2,1)} fusion(bf16[256,6144]{1,0:T(8,128)(2,1)} %all-gather.4.cloned.1.call-done, f32[64,1,256]{2,1,0:T(1,128)S(1)} %slice_convert_fusion, f32[256]{0:T(256)S(1)} %dynamic_slice.24, f32[64]{0:T(128)S(1)} %add_rsqrt_fusion), kind=kOutput, calls=%fused_computation.7 | convolution fusion | flops 201768960 | bytes 3998976 | tf_op jit(solution)/shard_map/dot_general | solution.py:138
  84.2 0.1 copy.140
  84.2 0.1 eq.31
  84.4 0.2 select_reduce_fusion.1
  84.6 0.1 reduce_sum.40
  84.7 0.1 copy.142
  84.8 0.1 fusion.36
  84.9 60.5 %reduce-scatter.3.cloned.1.call-done = bf16[8,6144]{1,0:T(8,128)(2,1)} async-done(((bf16[64,6144]{1,0:T(8,128)(2,1)}), bf16[8,6144]{1,0:T(8,128)(2,1)}) %reduce-scatter.3.cloned.1.call-update) | async-done | bytes 98320 | tf_op jit(solution)/shard_map/reduce_scatter | solution.py:143
  145.4 1.2 fusion.3
  146.6 21.7 %all_to_all.71 = bf16[8,8,6144]{2,1,0:T(8,128)(2,1)S(1)} all-to-all(bf16[8,8,6144]{2,1,0:T(8,128)(2,1)S(1)} %bitcast.98), channel_id=1, replica_groups=mesh['seg'=4,'ep'=8] {'ep'}, dimensions={0} | all-to-all | bytes 1572864 | tf_op jit(solution)/shard_map/all_to_all | solution.py:154
  168.4 11.4 %collective-permute-done = bf16[64,6144]{1,0:T(8,128)(2,1)S(1)} collective-permute-done((bf16[64,6144]{1,0:T(8,128)(2,1)S(1)}, bf16[64,6144]{1,0:T(8,128)(2,1)S(1)}, u32[]{:S(2)}, u32[]{:S(2)}) %collective-permute-start) | collective-permute-done | bytes 786464 | tf_op jit(solution)/shard_map/ppermute | solution.py:74
  179.8 11.4 %collective-permute-done.1 = bf16[64,6144]{1,0:T(8,128)(2,1)S(1)} collective-permute-done((bf16[64,6144]{1,0:T(8,128)(2,1)S(1)}, bf16[64,6144]{1,0:T(8,128)(2,1)S(1)}, u32[]{:S(2)}, u32[]{:S(2)}) %collective-permute-start.1) | collective-permute-done | bytes 786464 | tf_op jit(solution)/shard_map/ppermute | solution.py:74
  191.2 11.4 %collective-permute-done.2 = bf16[64,6144]{1,0:T(8,128)(2,1)S(1)} collective-permute-done((bf16[64,6144]{1,0:T(8,128)(2,1)S(1)}, bf16[64,6144]{1,0:T(8,128)(2,1)S(1)}, u32[]{:S(2)}, u32[]{:S(2)}) %collective-permute-start.2) | collective-permute-done | bytes 786464 | tf_op jit(solution)/shard_map/ppermute | solution.py:74
  202.6 0.9 constant_dynamic-update-slice_fusion.7
  203.6 1.0 constant_dynamic-update-slice_fusion.6
  204.5 0.9 constant_dynamic-update-slice_fusion.5
  205.5 0.9 constant_dynamic-update-slice_fusion.4
  206.4 0.9 constant_dynamic-update-slice_fusion.3
  207.3 0.9 constant_dynamic-update-slice_fusion.2
  208.3 0.9 constant_dynamic-update-slice_fusion.1
  209.2 1.0 constant_dynamic-update-slice_fusion
  210.2 15.9 %convolution_convert_fusion = bf16[256,6144]{1,0:T(8,128)(2,1)} fusion(bf16[1,576,6144]{2,1,0:T(8,128)(2,1)} %param.21, bf16[1,6144,576]{1,2,0:T(8,128)(2,1)} %param.20, bf16[512,6144]{1,0:T(8,128)(2,1)} %constant_dynamic-update-slice_fusion, s32[]{:T(128)S(6)} %select_n.44), kind=kOutput, calls=%fused_computation.3 | convolution fusion | flops 3626188800 | bytes 20447236 | tf_op jit(solution)/shard_map/dot_general | solution.py:57
  226.1 0.2 all_to_all.61
  226.3 11.8 %all_to_all.72 = bf16[8,64,256]{2,1,0:T(8,128)(2,1)S(1)} all-to-all(bf16[8,64,256]{2,1,0:T(8,128)(2,1)S(1)} %all_to_all.61), channel_id=1, replica_groups=mesh['seg'=4,'ep'=8] {'ep'}, dimensions={0} | all-to-all | bytes 524288 | tf_op jit(solution)/shard_map/all_to_all | solution.py:124
  238.1 25.1 %reduce-scatter.5.cloned.1.call-done = bf16[64,6144]{1,0:T(8,128)(2,1)} async-done(((bf16[256,6144]{1,0:T(8,128)(2,1)}), bf16[64,6144]{1,0:T(8,128)(2,1)}) %reduce-scatter.5.cloned.1.call-update) | async-done | bytes 786448 | tf_op jit(solution)/shard_map/reduce_scatter | solution.py:158
  263.2 5.5 %all-to-all-start.5 = ((bf16[8,8,6144]{2,1,0:T(8,128)(2,1)}), bf16[8,8,6144]{2,1,0:T(8,128)(2,1)S(1)}, u32[]{:S(2)}, u32[]{:S(2)}) async-start(bf16[8,8,6144]{2,1,0:T(8,128)(2,1)} %bitcast.105), calls=%async_computation.7 | async-start | bytes 1572864 | tf_op jit(solution)/shard_map/all_to_all | solution.py:164
  268.7 0.1 select_reduce_fusion
  268.9 0.2 fusion.21
  269.1 0.8 multiply_convert_fusion.2
  269.9 18.9 %all-to-all-done.5 = bf16[8,8,6144]{2,1,0:T(8,128)(2,1)S(1)} async-done(((bf16[8,8,6144]{2,1,0:T(8,128)(2,1)}), bf16[8,8,6144]{2,1,0:T(8,128)(2,1)S(1)}, u32[]{:S(2)}, u32[]{:S(2)}) %all-to-all-start.5) | async-done | bytes 786464 | tf_op jit(solution)/shard_map/all_to_all | solution.py:164
  288.8 0.1 convert.7
  288.9 1.2 convolution_convert_fusion.3
  (30 shorter events, 0.7 us)
Async XLA Ops:
  8.8 16.2 %all-to-all-start.1 = ((bf16[64,8,256]{2,0,1:T(8,128)(2,1)}), bf16[64,8,256]{2,0,1:T(8,128)(2,1)S(1)}, u32[]{:S(2)}, u32[]{:S(2)}) async-start(bf16[64,8,256]{2,0,1:T(8,128)(2,1)} %bitcast.88), calls=%async_computation.1 | async-start | bytes 524288 | tf_op jit(solution)/shard_map/all_to_all | solution.py:86
  25.0 12.2 %all-to-all-start.2 = ((bf16[64,8,256]{2,0,1:T(8,128)(2,1)}), bf16[64,8,256]{2,0,1:T(8,128)(2,1)S(1)}, u32[]{:S(2)}, u32[]{:S(2)}) async-start(bf16[64,8,256]{2,0,1:T(8,128)(2,1)} %bitcast.87), calls=%async_computation.2 | async-start | bytes 524288 | tf_op jit(solution)/shard_map/all_to_all | solution.py:87
  28.6 52.0 %all-gather.4.cloned.1.call-start = ((), (), s32[]{:S(2)}) async-start(), calls=%async_computation.8 | async-start | bytes 3932160 | tf_op jit(solution)/shard_map/all_gather | solution.py:140
  37.2 12.1 %all-to-all-start = ((bf16[64,8,256]{2,0,1:T(8,128)(2,1)}), bf16[64,8,256]{2,0,1:T(8,128)(2,1)S(1)}, u32[]{:S(2)}, u32[]{:S(2)}) async-start(bf16[64,8,256]{2,0,1:T(8,128)(2,1)} %bitcast.89), calls=%async_computation | async-start | bytes 524288 | tf_op jit(solution)/shard_map/all_to_all | solution.py:85
  40.8 104.6 %reduce-scatter.3.cloned.1.call-start = ((), (), s32[]{:S(2)}) async-start(), calls=%async_computation.9 | async-start | bytes 884736 | tf_op jit(solution)/shard_map/reduce_scatter | solution.py:143
  58.3 25.9 %copy-start.1 = (s32[8,2]{0,1:T(2,128)S(1)}, s32[8,2]{0,1:T(2,128)}, u32[]{:S(2)}) copy-start(s32[8,2]{0,1:T(2,128)} %param.18) | copy-start | bytes 196
  84.1 179.1 %reduce-scatter.5.cloned.1.call-start = ((), (), s32[]{:S(2)}) async-start(), calls=%async_computation.10 | async-start | bytes 3932160 | tf_op jit(solution)/shard_map/reduce_scatter | solution.py:158
  168.4 11.4 %collective-permute-start = (bf16[64,6144]{1,0:T(8,128)(2,1)S(1)}, bf16[64,6144]{1,0:T(8,128)(2,1)S(1)}, u32[]{:S(2)}, u32[]{:S(2)}) collective-permute-start(bf16[64,6144]{1,0:T(8,128)(2,1)S(1)} %bitcast.97), channel_id=1, source_target_pairs={{0,8},{8,16},{16,24},{24,0},{1,9},{9,17},{17,25},{25,1},{2,10},{10... | collective-permute-start | bytes 2359304 | tf_op jit(solution)/shard_map/ppermute | solution.py:74
  179.8 11.4 %collective-permute-start.1 = (bf16[64,6144]{1,0:T(8,128)(2,1)S(1)}, bf16[64,6144]{1,0:T(8,128)(2,1)S(1)}, u32[]{:S(2)}, u32[]{:S(2)}) collective-permute-start(bf16[64,6144]{1,0:T(8,128)(2,1)S(1)} %collective-permute-done), channel_id=1, source_target_pairs={{0,8},{8,16},{16,24},{24,0},{1,9},{9,17},{17,25},{25,1},{2,10},{10... | collective-permute-start | bytes 2359304 | tf_op jit(solution)/shard_map/ppermute | solution.py:74
  191.2 11.4 %collective-permute-start.2 = (bf16[64,6144]{1,0:T(8,128)(2,1)S(1)}, bf16[64,6144]{1,0:T(8,128)(2,1)S(1)}, u32[]{:S(2)}, u32[]{:S(2)}) collective-permute-start(bf16[64,6144]{1,0:T(8,128)(2,1)S(1)} %collective-permute-done.1), channel_id=1, source_target_pairs={{0,8},{8,16},{16,24},{24,0},{1,9},{9,17},{17,25},{25,1},{2,10},{10... | collective-permute-start | bytes 2359304 | tf_op jit(solution)/shard_map/ppermute | solution.py:74
  210.2 58.5 %copy-start.2 = (f32[8,2]{0,1:T(2,128)S(1)}, f32[8,2]{0,1:T(2,128)}, u32[]{:S(2)}) copy-start(f32[8,2]{0,1:T(2,128)} %param.19) | copy-start | bytes 196
  226.1 42.9 %copy-start = (f32[2048]{0:T(1024)S(1)}, f32[2048]{0:T(1024)}, u32[]{:S(2)}) copy-start(f32[2048]{0:T(1024)} %param.16) | copy-start | bytes 24580
  263.2 25.6 %all-to-all-start.5 = ((bf16[8,8,6144]{2,1,0:T(8,128)(2,1)}), bf16[8,8,6144]{2,1,0:T(8,128)(2,1)S(1)}, u32[]{:S(2)}, u32[]{:S(2)}) async-start(bf16[8,8,6144]{2,1,0:T(8,128)(2,1)} %bitcast.105), calls=%async_computation.7 | async-start | bytes 1572864 | tf_op jit(solution)/shard_map/all_to_all | solution.py:164
Sparse Core Ops, SparseCore 0:
  31.0 31.3 all-gather.3
  84.2 61.1 reduce-scatter.2
  226.2 36.8 reduce-scatter.4
